TPU v7x, 256 devices: a whole 4x4x8 slice. The times are simulated.
256 devices in a mesh: gz: 2 (over core), row: 4 (over x), col: 32 (over z, y).
Axes of the slice: x: 4, y: 4, z: 8, core: 2. Of those that a mesh axis runs over, the one named last changes fastest.
Arguments:
- ancestor: float32 [4096, 16384], P('row', 'col'), may hold values from -6 to 6
- lower_panel: bfloat16 [2, 64, 24, 128, 128], P('gz', 'col', 'row'), may hold values from -6 to 6
- row_ids: int32 [2, 64, 24], P('gz', 'col', 'row'), may hold values from 0 to 7, as said below
- row_counts: int32 [2, 64, 4], P('gz', 'col', 'row'), may hold values from 1 to 6
- diag_inverse: bfloat16 [2, 64, 128, 128], P('gz', 'col'), may hold values from -0.5 to 0.5
- upper_panel: bfloat16 [2, 64, 96, 128, 128], P('gz', 'row', 'col'), may hold values from -0.1875 to 0.1875
- col_ids: int32 [2, 64, 96], P('gz', 'row', 'col'), may hold values from 0 to 3, as said below
- col_counts: int32 [2, 64, 32], P('gz', 'row', 'col'), may hold values from 1 to 3
Outputs:
- updated: float32 [4096, 16384], P('row', 'col')
Inputs may be any that keep to these rules, and one draw needn't show every extreme that they name: `row_ids`: within each layer, supernode and process row the 6 slots name distinct local block rows. `col_ids`: within each layer, supernode and process column the 3 slots name distinct local block columns.
All inputs are finite; a program needn't handle non-finite values.
Results may differ from a plain program's by a relative error of at most 0.0026.
Values may be sent and summed in bfloat16 or wider, within the bound.
A program may use at most 128 MiB of HBM per device.

v0:
```python
import jax
import jax.numpy as jnp
from jax import lax
from jax.sharding import PartitionSpec as P


def spread_rows(tiles, ids, counts, blocks):
    slots = ids.shape[1]
    slot_index = jnp.arange(slots, dtype=jnp.int32)
    alive = slot_index[None, :] < counts
    target = jnp.arange(blocks, dtype=jnp.int32)
    select = ((ids[:, :, None] == target[None, None, :]) & alive[:, :, None]).astype(jnp.bfloat16)
    dense = jnp.einsum("krl,krab->lakb", select, tiles, preferred_element_type=jnp.float32).astype(
        jnp.bfloat16
    )
    width = tiles.shape[-1]
    return dense.reshape(blocks * width, tiles.shape[0] * width)


def spread_cols(tiles, ids, counts, blocks):
    slots = ids.shape[1]
    slot_index = jnp.arange(slots, dtype=jnp.int32)
    alive = slot_index[None, :] < counts
    target = jnp.arange(blocks, dtype=jnp.int32)
    select = ((ids[:, :, None] == target[None, None, :]) & alive[:, :, None]).astype(jnp.bfloat16)
    dense = jnp.einsum("kcm,kcab->kamb", select, tiles, preferred_element_type=jnp.float32).astype(
        jnp.bfloat16
    )
    width = tiles.shape[-1]
    return dense.reshape(tiles.shape[0] * width, blocks * width)


def on_device(
    ancestor, lower_panel, row_ids, row_counts, diag_inverse, upper_panel, col_ids, col_counts
):
    width = lower_panel.shape[-1]
    row_blocks = ancestor.shape[0] // width
    col_blocks = ancestor.shape[1] // width
    solved = jnp.einsum(
        "ksab,kbc->ksac", lower_panel[0], diag_inverse[0], preferred_element_type=jnp.float32
    ).astype(jnp.bfloat16)
    piece = lax.all_gather((upper_panel[0], col_ids[0], col_counts[0]), "row", axis=0, tiled=True)
    upper_dense = spread_cols(piece[0], piece[1], piece[2], col_blocks)
    piece = lax.all_gather((solved, row_ids[0], row_counts[0]), "col", axis=0, tiled=True)
    lower_dense = spread_rows(piece[0], piece[1], piece[2], row_blocks)
    partial_sum = jnp.dot(lower_dense, upper_dense, preferred_element_type=jnp.float32)
    return ancestor - lax.psum(partial_sum, "gz")


def solution(mesh):
    placed = (
        P("row", "col"),
        P("gz", "col", "row", None, None),
        P("gz", "col", "row"),
        P("gz", "col", "row"),
        P("gz", "col", None, None),
        P("gz", "row", "col", None, None),
        P("gz", "row", "col"),
        P("gz", "row", "col"),
    )
    return jax.shard_map(
        on_device, mesh=mesh, in_specs=placed, out_specs=P("row", "col"), check_vma=False
    )
```

profile of v0, /device:TPU:1, one launch (start us, length us, event | category | flops | bytes accessed | tf_op | source)
XLA Modules:
  0.0 301.7 jit_solution(158132594757815860)
XLA Ops:
  6.5 0.0 copy-start
  6.5 0.0 all-gather.10.cloned.1.call-start
  6.5 0.7 all-gather.10.cloned.1.call-update
  7.3 0.0 all-gather.8.cloned.1.call-start
  7.3 0.2 copy-done
  7.5 1.8 convolution_convert_fusion
  9.4 0.0 all-gather.8.cloned.1.call-update
  9.4 0.0 all-reduce.4.cloned.1.call-start
  9.4 1.3 dynamic-slice
  10.8 1.3 dynamic-slice.1
  12.1 0.8 copy.17
  14.2 0.8 bitcast_dynamic-update-slice_fusion.1
  14.9 20.0 %all-reduce = s32[64]{0:T(128)S(1)} all-reduce(s32[64]{0:T(128)S(1)} %bitcast_dynamic-update-slice_fusion.1), channel_id=3, replica_groups=mesh['gz'=2,'row'=4,'col'=32] {'col'}, use_global_device_ids=true, to_apply=%add | all-reduce | flops 64 | bytes 512
  35.0 0.7 bitcast_dynamic-update-slice_fusion
  35.7 7.7 %all-reduce.1 = s32[64]{0:T(128)S(1)} all-reduce(s32[64]{0:T(128)S(1)} %bitcast_dynamic-update-slice_fusion), channel_id=5, replica_groups=mesh['gz'=2,'row'=4,'col'=32] {'row'}, use_global_device_ids=true, to_apply=%add.1 | all-reduce | flops 64 | bytes 512
  43.4 10.6 %all-gather.2 = s32[1,64,3]{2,0,1:T(1,128)S(1)} all-gather(s32[1,16,3]{2,0,1:T(1,128)S(1)} %copy.17), channel_id=4, replica_groups=mesh['gz'=2,'row'=4,'col'=32] {'row'}, dimensions={1}, use_global_device_ids=true | all-gather | bytes 960 | tf_op jit(solution)/shard_map/all_gather | solution.py:42
  54.0 35.0 %all-gather = s32[1,64,6]{2,0,1:T(1,128)S(1)} all-gather(s32[1,2,6]{2,0,1:T(1,128)} %bitcast.51), channel_id=2, replica_groups=mesh['gz'=2,'row'=4,'col'=32] {'col'}, dimensions={1}, use_global_device_ids=true | all-gather | bytes 1584 | tf_op jit(solution)/shard_map/all_gather | solution.py:44
  89.1 0.1 iota_compare_fusion.3
  89.1 0.1 iota_compare_fusion.2
  89.2 0.0 all-gather.10.cloned.1.call-done
  89.2 11.1 %fusion.12 = bf16[64,4,128,128]{3,1,2,0:T(4,128)(2,1)} fusion(bf16[1,64,3,128,128]{4,3,2,0,1:T(8,128)(2,1)} %all-gather.10.cloned.1.call-done, s32[64,3]{1,0:T(8,128)S(1)} %bitcast.50, pred[64,3]{1,0:T(8,128)(4,1)S(1)} %iota_compare_fusion.2), kind=kOutput, calls=%fused_computation.11 | convolution fusion | flops 29361664 | bytes 14681024 | tf_op jit(solution)/shard_map/kcm,kcab->kamb/dot_general | solution.py:26
  100.3 102.7 %all-gather.8.cloned.1.call-done = bf16[64,6,128,128]{3,2,1,0:T(8,128)(2,1)} async-done(((bf16[2,6,128,128]{3,2,1,0:T(8,128)(2,1)}), bf16[64,6,128,128]{3,2,1,0:T(8,128)(2,1)}) %all-gather.8.cloned.1.call-update) | async-done | bytes 12582928 | tf_op jit(solution)/shard_map/all_gather | solution.py:44
  203.0 16.6 %convert_bitcast_fusion = bf16[8,128,64,128]{3,0,1,2:T(8,128)(2,1)} fusion(bf16[64,6,128,128]{3,2,1,0:T(8,128)(2,1)} %all-gather.8.cloned.1.call-done, s32[64,6]{1,0:T(8,128)S(1)} %bitcast.49, pred[64,6]{1,0:T(8,128)(4,1)S(1)} %iota_compare_fusion.3), kind=kOutput, calls=%fused_computation.5 | convolution fusion | flops 109058048 | bytes 29362048 | tf_op jit(solution)/shard_map/krl,krab->lakb/dot_general | solution.py:13
  219.7 0.0 copy-start.3
  219.7 18.9 %copy.16 = bf16[8,128,64,128]{3,2,1,0:T(8,128)(2,1)} copy(bf16[8,128,64,128]{3,0,1,2:T(8,128)(2,1)} %convert_bitcast_fusion) | data formatting | bytes 33554432 | tf_op jit(solution)/shard_map/convert_element_type | solution.py:13
  238.6 0.0 copy-done.3
  238.6 22.4 %fusion = f32[1024,512]{1,0:T(8,128)} fusion(bf16[128,8,64,128]{3,2,1,0:T(8,128)(2,1)} %bitcast.47, bf16[1024,8,4,128]{3,2,1,0:T(4,128)(2,1)S(1)} %bitcast.52), kind=kOutput, calls=%fused_computation | convolution fusion | flops 8589934592 | bytes 27262976 | tf_op jit(solution)/shard_map/dot_general | solution.py:46
  261.0 0.0 all-reduce.4.cloned.1.call-update
  261.0 30.8 %all-reduce.4.cloned.1.call-done = f32[1024,512]{1,0:T(8,128)} async-done(((f32[1024,512]{1,0:T(8,128)}), f32[1024,512]{1,0:T(8,128)}) %all-reduce.4.cloned.1.call-update) | async-done | bytes 2097168 | tf_op jit(solution)/shard_map/psum | solution.py:47
  291.8 0.0 copy-done.2
  291.8 3.4 %sub.3 = f32[1024,512]{1,0:T(8,128)} subtract(f32[1024,512]{1,0:T(8,128)S(1)} %copy-done.2, f32[1024,512]{1,0:T(8,128)} %all-reduce.4.cloned.1.call-done) | non-fusion elementwise | flops 524288 | bytes 6291456 | tf_op jit(solution)/shard_map/sub | solution.py:47
  295.2 0.0 copy-done.1
  (4 shorter events, 0.0 us)
Async XLA Ops:
  6.5 1.0 copy-start
  6.5 82.7 %all-gather.10.cloned.1.call-start = ((), (), s32[]{:S(2)}) async-start(), calls=%async_computation.2 | async-start | bytes 7864320 | tf_op jit(solution)/shard_map/all_gather | solution.py:42
  7.3 195.8 %all-gather.8.cloned.1.call-start = ((), (), s32[]{:S(2)}) async-start(), calls=%async_computation | async-start | bytes 12976128 | tf_op jit(solution)/shard_map/all_gather | solution.py:44
  9.4 282.4 %all-reduce.4.cloned.1.call-start = ((), (), s32[]{:S(2)}) async-start(), calls=%async_computation.1 | async-start | bytes 4194304 | tf_op jit(solution)/shard_map/psum | solution.py:47
  219.7 18.9 %copy-start.3 = (bf16[64,4,128,128]{3,1,2,0:T(4,128)(2,1)S(1)}, bf16[64,4,128,128]{3,1,2,0:T(4,128)(2,1)}, u32[]{:S(2)}) copy-start(bf16[64,4,128,128]{3,1,2,0:T(4,128)(2,1)} %fusion.12) | copy-start | bytes 25165828
  238.6 53.2 %copy-start.2 = (f32[1024,512]{1,0:T(8,128)S(1)}, f32[1024,512]{1,0:T(8,128)}, u32[]{:S(2)}) copy-start(f32[1024,512]{1,0:T(8,128)} %param.8) | copy-start | bytes 6291460
  238.6 56.6 %copy-start.1 = (bf16[1,2,6,128,128]{4,3,2,1,0:T(8,128)(2,1)S(1)}, bf16[1,2,6,128,128]{4,3,2,1,0:T(8,128)(2,1)}, u32[]{:S(2)}) copy-start(bf16[1,2,6,128,128]{4,3,2,1,0:T(8,128)(2,1)} %param.9) | copy-start | bytes 1179652
Sparse Core Ops, SparseCore 0:
  9.1 72.1 all-gather.9
  83.9 119.0 all-gather.7
  261.1 30.5 all-reduce.3
where the time goes:
time: 302 us
  waiting for transfers between devices  134 us (44%)
  blocking collectives  73.4 us (24%)
  matrix products  52 us (17%)
  local copies, waits for them, and re-layouts  24.1 us (8%)
  between operations  14.5 us (5%)
  other arithmetic  3.53 us (1%)
    all_gather x1, waiting for transfers between devices, on_device(): lax.all_gather((solved, row_ids[0], row_counts[0]), 'col', axis=0, tiled=...  103 us
    all_gather x1, blocking collectives, on_device(): lax.all_gather((solved, row_ids[0], row_counts[0]), 'col', axis=0, tiled=...  35 us
    psum x1, waiting for transfers between devices, on_device(): return ancestor - lax.psum(partial_sum, 'gz')  30.8 us
    unnamed x2, blocking collectives  27.7 us
    dot_general x1, matrix products, on_device(): jnp.dot(lower_dense, upper_dense, preferred_element_type=jnp.float32)  22.4 us
    convert_element_type x1, local copies, waits for them, and re-layouts, spread_rows(): jnp.einsum('krl,krab->lakb', select, tiles, preferred_element_type=jnp.fl...  18.9 us
    dot_general x1, matrix products, spread_rows(): jnp.einsum('krl,krab->lakb', select, tiles, preferred_element_type=jnp.fl...  16.6 us
    dot_general x1, matrix products, spread_cols(): jnp.einsum('kcm,kcab->kamb', select, tiles, preferred_element_type=jnp.fl...  11.1 us
  transfers between devices with their start and end apart: 3, of which 2 were waited for; matrix products, arithmetic and copies ran while one was open for 6% of the time, Pallas kernels for 0%

commit v1 on v0

v1 whole, which is shorter than its diff:
```python
import jax
import jax.numpy as jnp
from jax import lax
from jax.experimental import pallas as pl
from jax.experimental.pallas import tpu as pltpu
from jax.sharding import PartitionSpec as P

B = 128
RL = 6
CL = 3
RB = 8
CB = 4
NX, NY, NZ = 4, 4, 8
DEPTH = 16 * B
HALF = RB * B // 2
WIDE = CB * B
N_COPIES = 96
N_LOCAL = 16


def mod(value, size):
    return lax.rem(value + 2 * size, size)


def kernel(
    rid, rcnt, cid, ccnt, anc, low, dinv, up, out,
    lowv, dinvv, ancv, own_meta, relay_meta, meta_l, meta_u, ids_l, ids_u,
    lbuf, ubuf, relay_u, ld, ud, part_out, part_own, gz_in, c_out, c_in, c_relay, fin,
    send_sem, recv_sem, local_sem,
):
    g = lax.axis_index("gz")
    x = lax.axis_index("row")
    col = lax.axis_index("col")
    z = lax.div(col, NY)
    y = lax.rem(col, NY)
    f32, bf16 = jnp.float32, jnp.bfloat16

    xs = {d: mod(x + d, NX) for d in (-1, 1, 2)}
    ys = {d: mod(y + d, NY) for d in (-1, 1, 2)}
    zs = {d: mod(z + d, NZ) for d in (-3, -2, -1, 1, 2, 3, 4)}
    xs[0], ys[0], zs[0] = x, y, z

    def place(axis, d):
        if axis == "x":
            return {"gz": g, "row": xs[d], "col": col}
        if axis == "y":
            return {"gz": g, "row": x, "col": z * NY + ys[d]}
        if axis == "z":
            return {"gz": g, "row": x, "col": zs[d] * NY + y}
        return {"gz": 1 - g, "row": x, "col": col}

    started = []
    count = [0]
    locals_started = [0]

    class Copy:
        def __init__(self, src, dst, axis, d):
            at = count[0]
            count[0] += 1
            self.copy = pltpu.make_async_remote_copy(
                src_ref=src, dst_ref=dst, send_sem=send_sem.at[at], recv_sem=recv_sem.at[at],
                device_id=place(axis, d), device_id_type=pl.DeviceIdType.MESH,
            )
            self.copy.start()
            started.append(self.copy)

        def arrived(self):
            self.copy.wait_recv()

    def local(src, dst):
        copy = pltpu.make_async_copy(src, dst, local_sem.at[locals_started[0]])
        locals_started[0] += 1
        copy.start()
        return copy

    mine = pl.ds(pl.multiple_of(g * HALF, HALF), HALF)
    theirs = pl.ds(pl.multiple_of((1 - g) * HALF, HALF), HALF)

    get_low = local(low, lowv)
    get_dinv = local(dinv, dinvv)
    get_up = local(up.at[:, y], ubuf.at[y, x])
    get_anc = local(anc.at[mine], ancv)

    barrier = pltpu.get_barrier_semaphore()
    for axis, d in (("x", 1), ("x", -1), ("y", 1), ("y", -1), ("z", 1), ("z", -1), ("g", 1)):
        pl.semaphore_signal(barrier, 1, device_id=place(axis, d), device_id_type=pl.DeviceIdType.MESH)

    lane = lax.broadcasted_iota(jnp.int32, (1, B), 1)
    row_list = jnp.full((1, B), RB, jnp.int32)
    for b in range(2):
        for s in range(RL):
            value = jnp.where(s < rcnt[b, 0], rid[b, s], RB)
            row_list = jnp.where(lane == b * RL + s, value, row_list)
    meta_l[z] = row_list
    for q in range(NY):
        col_list = jnp.full((1, B), CB, jnp.int32)
        for zz in range(2):
            for b in range(2):
                k = zz * 8 + q * 2 + b
                for s in range(CL):
                    value = jnp.where(s < ccnt[k, 0], cid[k, s], CB)
                    col_list = jnp.where(lane == (zz * 2 + b) * CL + s, value, col_list)
        own_meta[q] = col_list
    meta_u[x, y] = own_meta[y]

    get_low.wait()
    get_dinv.wait()
    for b in range(2):
        solved = jnp.dot(
            lowv[b].reshape(RL * B, B), dinvv[b], preferred_element_type=f32
        ).astype(bf16)
        lbuf[z, b] = solved.reshape(RL, B, B)

    pl.semaphore_wait(barrier, 7)

    both = (1, -1)
    half_of = {1: 0, -1: 1}
    my = {d: Copy(own_meta.at[ys[d]], meta_u.at[x, y], "y", d) for d in both}
    my_far = Copy(own_meta.at[ys[2]], relay_meta, "y", 1)
    ml = {(d, 0): Copy(meta_l.at[z], meta_l.at[z], "z", d) for d in both}
    yr = {d: Copy(up.at[half_of[d], ys[2]], relay_u.at[half_of[d]], "y", d) for d in both}
    lz = {(d, 0, b): Copy(lbuf.at[z, b], lbuf.at[z, b], "z", d) for b in range(2) for d in both}
    xo = {}
    for h in range(2):
        for d in both:
            xo[d, 0, h] = Copy(up.at[h, y], ubuf.at[y, x, h], "x", d)
    yd = {
        (d, h): Copy(up.at[h, ys[d]], ubuf.at[y, x, h], "y", d) for h in range(2) for d in both
    }
    get_up.wait()

    def forward_list(d, hop):
        ml[d, hop] = Copy(meta_l.at[zs[-d * hop]], meta_l.at[zs[-d * hop]], "z", d)

    def forward_lower(d, hop, b):
        lz[d, hop, b] = Copy(lbuf.at[zs[-d * hop], b], lbuf.at[zs[-d * hop], b], "z", d)

    def along_x(block, h):
        for d in both:
            xo[d, block, h] = Copy(ubuf.at[ys[block], x, h], ubuf.at[ys[block], x, h], "x", d)

    xf = {}

    def onward_x(block):
        for d in both:
            h = half_of[d]
            xf[d, block] = Copy(
                ubuf.at[ys[block], xs[-d], h], ubuf.at[ys[block], xs[-d], h], "x", d
            )

    for d in both:
        my[d].arrived()
        ml[d, 0].arrived()
        forward_list(d, 1)
    my_far.arrived()
    far_list = Copy(relay_meta, meta_u.at[x, ys[-1]], "y", 1)
    for d in both:
        lz[d, 0, 0].arrived()
        forward_lower(d, 1, 0)
    yrf = {}
    for d in both:
        yr[d].arrived()
        yrf[d] = Copy(relay_u.at[half_of[d]], ubuf.at[ys[-d], x, half_of[d]], "y", d)
    for d in both:
        ml[d, 1].arrived()
        forward_list(d, 2)
        lz[d, 0, 1].arrived()
        forward_lower(d, 1, 1)
    far_list.arrived()
    mx = {d: Copy(meta_u.at[x], meta_u.at[x], "x", d) for d in both}
    yd[1, 0].arrived()
    yd[-1, 0].arrived()
    along_x(-1, 0)
    along_x(1, 0)
    for d in both:
        lz[d, 1, 0].arrived()
        forward_lower(d, 2, 0)
        ml[d, 2].arrived()
    forward_list(1, 3)
    yd[1, 1].arrived()
    yd[-1, 1].arrived()
    along_x(-1, 1)
    along_x(1, 1)
    for d in both:
        mx[d].arrived()
    mx_far = Copy(meta_u.at[xs[-1]], meta_u.at[xs[-1]], "x", 1)
    for d in both:
        lz[d, 1, 1].arrived()
        forward_lower(d, 2, 1)
    for d in both:
        yrf[d].arrived()
    for d in both:
        lz[d, 2, 0].arrived()
    forward_lower(1, 3, 0)
    ml[1, 3].arrived()
    get_ids_l = local(meta_l, ids_l)
    for h in range(2):
        for d in both:
            xo[d, -1, h].arrived() if h == 0 else None
    for d in both:
        xo[d, 1, 0].arrived()
    for d in both:
        xo[d, -1, 1].arrived()
    onward_x(-1)
    for d in both:
        lz[d, 2, 1].arrived()
    forward_lower(-1, 3, 1)
    mx_far.arrived()
    get_ids_u = local(meta_u, ids_u)
    for d in both:
        xo[d, 1, 1].arrived()
    onward_x(1)
    along_x(2, 0)
    along_x(2, 1)
    for d in both:
        for h in range(2):
            xo[d, 0, h].arrived()
    get_ids_l.wait()
    lz[1, 3, 0].arrived()
    lz[-1, 3, 1].arrived()

    @pl.loop(0, NZ)
    def _(zi):
        for b in range(2):
            ids = [ids_l[zi, 0, b * RL + s] for s in range(RL)]
            at = pl.ds(pl.multiple_of(zi * 2 * B + b * B, B), B)
            for i in range(RB):
                tile = jnp.zeros((B, B), bf16)
                for s in range(RL):
                    tile = lax.select(ids[s] == i, lbuf[zi, b, s], tile)
                ld[i * B : (i + 1) * B, at] = tile

    get_ids_u.wait()

    def spread_upper(block, xi):
        for h in range(2):
            for b in range(2):
                k = h * 2 + b
                ids = [ids_u[xi, block, 0, k * CL + s] for s in range(CL)]
                at = pl.ds(pl.multiple_of(xi * 4 * B + k * B, B), B)
                for j in range(CB):
                    tile = jnp.zeros((B, B), bf16)
                    for s in range(CL):
                        tile = lax.select(ids[s] == j, ubuf[block, xi, h, b * CL + s], tile)
                    ud[at, j * B : (j + 1) * B] = tile

    def multiply(rows):
        return jnp.dot(ld[rows, :], ud[...], preferred_element_type=f32)

    gz = {}

    def contribute(block, at):
        @pl.loop(0, NX)
        def _(xi):
            spread_upper(ys[block], xi)

        part_out[at] = multiply(theirs)
        part_own[at] = multiply(mine)
        gz[at] = Copy(part_out.at[at], gz_in.at[at], "g", 1)

    cs = {}

    def settle(block, at):
        gz[at].arrived()
        c_out[at] = (part_own[at] + gz_in[at]).astype(bf16)
        if block == 2:
            for d in both:
                for n in range(2):
                    rows = pl.ds((2 * half_of[d] + n) * B, B)
                    cs[d, n] = Copy(c_out.at[at, rows], c_relay.at[rows], "y", d)
        else:
            cs[block] = Copy(c_out.at[at], c_in.at[at], "y", block)

    for d in both:
        xf[d, -1].arrived()
    contribute(-1, 0)
    for d in both:
        for h in range(2):
            xo[d, 2, h].arrived()
    onward_x(2)
    onward_x(0)
    for d in both:
        xf[d, 1].arrived()
    settle(-1, 0)
    contribute(1, 1)
    settle(1, 1)

    for d in both:
        xf[d, 2].arrived()
    contribute(2, 2)
    settle(2, 2)
    for d in both:
        xf[d, 0].arrived()
    contribute(0, 3)

    cf = {}
    for n in range(2):
        for d in both:
            rows = pl.ds((2 * half_of[d] + n) * B, B)
            cs[d, n].arrived()
            cf[d, n] = Copy(c_relay.at[rows], c_in.at[2, rows], "y", d)
    gz[3].arrived()
    cs[-1].arrived()
    cs[1].arrived()
    get_anc.wait()
    fin[...] = ancv[...] - (part_own[3] + gz_in[3] + c_in[0].astype(f32) + c_in[1].astype(f32))
    last = []
    stores = []
    for n in range(2):
        for d in both:
            begin = (2 * half_of[d] + n) * B
            rows = pl.ds(begin, B)
            there = pl.ds(pl.multiple_of(g * HALF + begin, B), B)
            cf[d, n].arrived()
            fin[rows] = fin[rows] - c_in[2, rows].astype(f32)
            stores.append(local(fin.at[rows], out.at[there]))
            last.append(Copy(fin.at[rows], out.at[there], "g", 1))
    for copy in last:
        copy.arrived()
    for store in stores:
        store.wait()
    for copy in started:
        copy.wait_send()


def on_device(
    ancestor, lower_panel, row_ids, row_counts, diag_inverse, upper_panel, col_ids, col_counts
):
    bf16, f32, i32 = jnp.bfloat16, jnp.float32, jnp.int32
    anywhere = pl.BlockSpec(memory_space=pl.ANY)
    scalars = pl.BlockSpec(memory_space=pltpu.SMEM)
    vmem = pltpu.VMEM
    return pl.pallas_call(
        kernel,
        out_shape=jax.ShapeDtypeStruct(ancestor.shape, f32),
        in_specs=[scalars] * 4 + [anywhere] * 4,
        out_specs=anywhere,
        scratch_shapes=[
            vmem((2, RL, B, B), bf16),
            vmem((2, B, B), bf16),
            vmem((HALF, WIDE), f32),
            vmem((NY, 1, B), i32),
            vmem((1, B), i32),
            vmem((NZ, 1, B), i32),
            vmem((NX, NY, 1, B), i32),
            pltpu.SMEM((NZ, 1, B), i32),
            pltpu.SMEM((NX, NY, 1, B), i32),
            vmem((NZ, 2, RL, B, B), bf16),
            vmem((NY, NX, 2, 2 * CL, B, B), bf16),
            vmem((2, 2 * CL, B, B), bf16),
            vmem((RB * B, DEPTH), bf16),
            vmem((DEPTH, WIDE), bf16),
            vmem((4, HALF, WIDE), f32),
            vmem((4, HALF, WIDE), f32),
            vmem((4, HALF, WIDE), f32),
            vmem((3, HALF, WIDE), bf16),
            vmem((3, HALF, WIDE), bf16),
            vmem((HALF, WIDE), bf16),
            vmem((HALF, WIDE), f32),
            pltpu.SemaphoreType.DMA((N_COPIES,)),
            pltpu.SemaphoreType.DMA((N_COPIES,)),
            pltpu.SemaphoreType.DMA((N_LOCAL,)),
        ],
        compiler_params=pltpu.CompilerParams(
            collective_id=0, has_side_effects=True, vmem_limit_bytes=60 * 1024 * 1024
        ),
        name="schur_update",
    )(
        row_ids[0], row_counts[0], col_ids[0], col_counts[0],
        ancestor, lower_panel[0], diag_inverse[0],
        upper_panel[0].reshape(2, NY, 2 * CL, B, B),
    )


def solution(mesh):
    placed = (
        P("row", "col"),
        P("gz", "col", "row", None, None),
        P("gz", "col", "row"),
        P("gz", "col", "row"),
        P("gz", "col", None, None),
        P("gz", "row", "col", None, None),
        P("gz", "row", "col"),
        P("gz", "row", "col"),
    )
    return jax.shard_map(
        on_device, mesh=mesh, in_specs=placed, out_specs=P("row", "col"), check_vma=False
    )
```

time: 302 us -> 100 us (0.33)
  waiting for transfers between devices: 134 us -> 0 us
  Pallas kernels: 0 us -> 93.1 us
  blocking collectives: 73.4 us -> 0 us
  matrix products: 52 us -> 0 us
  local copies, waits for them, and re-layouts: 24.1 us -> 7.07 us
  between operations: 14.5 us -> 0.01 us
  other arithmetic: 3.53 us -> 0 us
    all_gather x2 -> x0, waiting for transfers between devices: 103 us -> none  [the longest x1 103 us: on_device(): lax.all_gather((solved, row_ids[0], row_counts[0]), 'col', axis=0, tiled=...]
    pallas_call x0 -> x1, Pallas kernels: none -> 93.1 us  [on_device(): pl.pallas_call(kernel, out_shape=jax.ShapeDtypeStruct(ancestor.shape, f32...]
    dot_general x4 -> x0, matrix products: 52 us -> none  [the longest x1 22.4 us: on_device(): jnp.dot(lower_dense, upper_dense, preferred_element_type=jnp.float32)]
    all_gather x2 -> x0, blocking collectives: 45.6 us -> none  [the longest x1 35 us: on_device(): lax.all_gather((solved, row_ids[0], row_counts[0]), 'col', axis=0, tiled=...]
    psum x1 -> x0, waiting for transfers between devices: 30.8 us -> none  [on_device(): return ancestor - lax.psum(partial_sum, 'gz')]
    unnamed x2 -> x0, blocking collectives: 27.7 us -> none
    convert_element_type x1 -> x0, local copies, waits for them, and re-layouts: 18.9 us -> none  [spread_rows(): jnp.einsum('krl,krab->lakb', select, tiles, preferred_element_type=jnp.fl...]
    squeeze x0 -> x3, local copies, waits for them, and re-layouts: none -> 3.99 us  [the longest x1 1.35 us: on_device(): col_ids[0]]
  transfers between devices with their start and end apart: 3 -> 0, of which waited for: 2 -> 0; matrix products, arithmetic and copies ran while one was open for 6% -> 0% of each run, Pallas kernels for 0% -> 0%
where the time goes in v1:
time: 100 us
  Pallas kernels  93.1 us (93%)
  local copies, waits for them, and re-layouts  7.07 us (7%)
    pallas_call x1, Pallas kernels, on_device(): pl.pallas_call(kernel, out_shape=jax.ShapeDtypeStruct(ancestor.shape, f32...  93.1 us
    unnamed x1, local copies, waits for them, and re-layouts  3.08 us

profile of v1, /device:TPU:1, one launch (start us, length us, event | category | flops | bytes accessed | tf_op | source)
XLA Modules:
  0.0 100.1 jit_solution(10934920045931877726)
XLA Ops:
  0.0 1.3 %copy.9.rcnt = s32[2,1]{1,0:T(2,128)} copy(s32[2,1]{0,1:T(1,128)} %bitcast.13) | data formatting | bytes 16 | tf_op jit(solution)/shard_map/squeeze | solution.py:369
  1.3 1.4 %copy.12 = s32[1,16,3]{2,1,0:T(8,128)} copy(s32[1,16,3]{1,0,2:T(1,128)} %param.14) | data formatting | bytes 384 | tf_op jit(solution)/shard_map/squeeze | solution.py:369
  2.7 1.3 %copy.11.ccnt = s32[16,1]{1,0:T(8,128)} copy(s32[16,1]{0,1:T(1,128)} %bitcast.12) | data formatting | bytes 128 | tf_op jit(solution)/shard_map/squeeze | solution.py:369
  4.0 93.1 %schur_update.1 = f32[1024,512]{1,0:T(8,128)} custom-call(s32[2,6]{1,0:T(2,128)} %bitcast.11, s32[2,1]{1,0:T(2,128)} %copy.9.rcnt, s32[16,3]{1,0:T(8,128)} %bitcast.10, s32[16,1]{1,0:T(8,128)} %copy.11.ccnt, f32[1024,512]{1,0:T(8,128)} %anc.1, bf16[2,6,128,128]{3,2,1,0:T(8,128)(2,1)} %bitcast.8, bf16[2,128,128]{2,1,0:T(8,128)(2,1)} %bitcast.9, ...), custom_call_target="tpu_custom_call" | custom-call | tf_op jit(solution)/shard_map/schur_update/pallas_call | solution.py:333
  97.1 3.1 %copy.14 = f32[1024,512]{1,0:T(8,128)} copy(f32[1024,512]{1,0:T(8,128)} %schur_update.1) | data formatting | bytes 4194304

commit v2 on v1

--- a/solution.py
+++ b/solution.py
@@ -14,7 +14,7 @@
 DEPTH = 16 * B
 HALF = RB * B // 2
 WIDE = CB * B
-N_COPIES = 96
+N_COPIES = 112
 N_LOCAL = 16
 
 
@@ -89,7 +89,7 @@
     row_list = jnp.full((1, B), RB, jnp.int32)
     for b in range(2):
         for s in range(RL):
-            value = jnp.where(s < rcnt[b, 0], rid[b, s], RB)
+            value = jnp.where(s < rcnt[0, b], rid[b, s], RB)
             row_list = jnp.where(lane == b * RL + s, value, row_list)
     meta_l[z] = row_list
     for q in range(NY):
@@ -98,10 +98,28 @@
             for b in range(2):
                 k = zz * 8 + q * 2 + b
                 for s in range(CL):
-                    value = jnp.where(s < ccnt[k, 0], cid[k, s], CB)
+                    value = jnp.where(s < ccnt[0, k], cid[s, 0, k], CB)
                     col_list = jnp.where(lane == (zz * 2 + b) * CL + s, value, col_list)
         own_meta[q] = col_list
     meta_u[x, y] = own_meta[y]
+
+
+    pl.semaphore_wait(barrier, 7)
+
+    both = (1, -1)
+    half_of = {1: 0, -1: 1}
+    my = {d: Copy(own_meta.at[ys[d]], meta_u.at[x, y], "y", d) for d in both}
+    my_far = Copy(own_meta.at[ys[2]], relay_meta, "y", 1)
+    ml = {(d, 0): Copy(meta_l.at[z], meta_l.at[z], "z", d) for d in both}
+    xo, xf, yd = {}, {}, {}
+    for d in both:
+        h = half_of[d]
+        xo[d, 0, h] = Copy(up.at[h, y], ubuf.at[y, x, h], "x", d)
+        yd[d, 0] = Copy(up.at[1 - h, ys[d]], ubuf.at[y, x, 1 - h], "y", d)
+    own_late = {}
+    for d in both:
+        h = 1 - half_of[d]
+        xo[d, 0, h] = Copy(up.at[h, y, 0:CL], ubuf.at[y, x, h, 0:CL], "x", d)
 
     get_low.wait()
     get_dinv.wait()
@@ -110,23 +128,13 @@
             lowv[b].reshape(RL * B, B), dinvv[b], preferred_element_type=f32
         ).astype(bf16)
         lbuf[z, b] = solved.reshape(RL, B, B)
-
-    pl.semaphore_wait(barrier, 7)
-
-    both = (1, -1)
-    half_of = {1: 0, -1: 1}
-    my = {d: Copy(own_meta.at[ys[d]], meta_u.at[x, y], "y", d) for d in both}
-    my_far = Copy(own_meta.at[ys[2]], relay_meta, "y", 1)
-    ml = {(d, 0): Copy(meta_l.at[z], meta_l.at[z], "z", d) for d in both}
+    lz = {(d, 0, b): Copy(lbuf.at[z, b], lbuf.at[z, b], "z", d) for b in range(2) for d in both}
+    my_far.arrived()
+    far_list = Copy(relay_meta, meta_u.at[x, ys[-1]], "y", 1)
+    for d in both:
+        h = half_of[d]
+        yd[d, 1] = Copy(up.at[h, ys[d]], ubuf.at[y, x, h], "y", d)
     yr = {d: Copy(up.at[half_of[d], ys[2]], relay_u.at[half_of[d]], "y", d) for d in both}
-    lz = {(d, 0, b): Copy(lbuf.at[z, b], lbuf.at[z, b], "z", d) for b in range(2) for d in both}
-    xo = {}
-    for h in range(2):
-        for d in both:
-            xo[d, 0, h] = Copy(up.at[h, y], ubuf.at[y, x, h], "x", d)
-    yd = {
-        (d, h): Copy(up.at[h, ys[d]], ubuf.at[y, x, h], "y", d) for h in range(2) for d in both
-    }
     get_up.wait()
 
     def forward_list(d, hop):
@@ -135,92 +143,77 @@
     def forward_lower(d, hop, b):
         lz[d, hop, b] = Copy(lbuf.at[zs[-d * hop], b], lbuf.at[zs[-d * hop], b], "z", d)
 
-    def along_x(block, h):
-        for d in both:
-            xo[d, block, h] = Copy(ubuf.at[ys[block], x, h], ubuf.at[ys[block], x, h], "x", d)
-
-    xf = {}
-
-    def onward_x(block):
-        for d in both:
-            h = half_of[d]
-            xf[d, block] = Copy(
-                ubuf.at[ys[block], xs[-d], h], ubuf.at[ys[block], xs[-d], h], "x", d
-            )
+    def along_x(d, block, h):
+        xo[d, block, h] = Copy(ubuf.at[ys[block], x, h], ubuf.at[ys[block], x, h], "x", d)
+
+    def onward_x(d, block):
+        h = half_of[d]
+        xo[d, block, h].arrived()
+        xf[d, block] = Copy(ubuf.at[ys[block], xs[-d], h], ubuf.at[ys[block], xs[-d], h], "x", d)
 
     for d in both:
         my[d].arrived()
         ml[d, 0].arrived()
         forward_list(d, 1)
-    my_far.arrived()
-    far_list = Copy(relay_meta, meta_u.at[x, ys[-1]], "y", 1)
     for d in both:
         lz[d, 0, 0].arrived()
         forward_lower(d, 1, 0)
-    yrf = {}
-    for d in both:
-        yr[d].arrived()
-        yrf[d] = Copy(relay_u.at[half_of[d]], ubuf.at[ys[-d], x, half_of[d]], "y", d)
+    for d in both:
+        yd[d, 0].arrived()
+        along_x(-d, -d, 1 - half_of[d])
+    far_list.arrived()
+    mx = {d: Copy(meta_u.at[x], meta_u.at[x], "x", d) for d in both}
     for d in both:
         ml[d, 1].arrived()
         forward_list(d, 2)
         lz[d, 0, 1].arrived()
         forward_lower(d, 1, 1)
-    far_list.arrived()
-    mx = {d: Copy(meta_u.at[x], meta_u.at[x], "x", d) for d in both}
-    yd[1, 0].arrived()
-    yd[-1, 0].arrived()
-    along_x(-1, 0)
-    along_x(1, 0)
+    for d in both:
+        yd[d, 1].arrived()
+    for d in both:
+        along_x(d, -d, half_of[d])
+    for d in both:
+        along_x(d, d, 1 - half_of[d])
+    for d in both:
+        mx[d].arrived()
+    mx_far = Copy(meta_u.at[xs[-1]], meta_u.at[xs[-1]], "x", 1)
+    for d in both:
+        along_x(d, -d, 1 - half_of[d])
     for d in both:
         lz[d, 1, 0].arrived()
         forward_lower(d, 2, 0)
         ml[d, 2].arrived()
     forward_list(1, 3)
-    yd[1, 1].arrived()
-    yd[-1, 1].arrived()
-    along_x(-1, 1)
-    along_x(1, 1)
-    for d in both:
-        mx[d].arrived()
-    mx_far = Copy(meta_u.at[xs[-1]], meta_u.at[xs[-1]], "x", 1)
+    yrf = {}
+    for d in both:
+        yr[d].arrived()
+        yrf[d] = Copy(relay_u.at[half_of[d]], ubuf.at[ys[-d], x, half_of[d]], "y", d)
+    for d in both:
+        onward_x(d, d)
     for d in both:
         lz[d, 1, 1].arrived()
         forward_lower(d, 2, 1)
     for d in both:
+        onward_x(d, -d)
+    for d in both:
         yrf[d].arrived()
+    for d in both:
+        along_x(d, 2, half_of[d])
+    for d in both:
+        along_x(d, 2, 1 - half_of[d])
     for d in both:
         lz[d, 2, 0].arrived()
     forward_lower(1, 3, 0)
     ml[1, 3].arrived()
     get_ids_l = local(meta_l, ids_l)
-    for h in range(2):
-        for d in both:
-            xo[d, -1, h].arrived() if h == 0 else None
-    for d in both:
-        xo[d, 1, 0].arrived()
-    for d in both:
-        xo[d, -1, 1].arrived()
-    onward_x(-1)
     for d in both:
         lz[d, 2, 1].arrived()
     forward_lower(-1, 3, 1)
     mx_far.arrived()
     get_ids_u = local(meta_u, ids_u)
-    for d in both:
-        xo[d, 1, 1].arrived()
-    onward_x(1)
-    along_x(2, 0)
-    along_x(2, 1)
-    for d in both:
-        for h in range(2):
-            xo[d, 0, h].arrived()
     get_ids_l.wait()
-    lz[1, 3, 0].arrived()
-    lz[-1, 3, 1].arrived()
-
-    @pl.loop(0, NZ)
-    def _(zi):
+
+    def spread_lower(zi):
         for b in range(2):
             ids = [ids_l[zi, 0, b * RL + s] for s in range(RL)]
             at = pl.ds(pl.multiple_of(zi * 2 * B + b * B, B), B)
@@ -229,6 +222,10 @@
                 for s in range(RL):
                     tile = lax.select(ids[s] == i, lbuf[zi, b, s], tile)
                 ld[i * B : (i + 1) * B, at] = tile
+
+    @pl.loop(1, NZ)
+    def _(hop):
+        spread_lower(mod(z + hop - 4 - NZ, NZ))
 
     get_ids_u.wait()
 
@@ -247,7 +244,12 @@
     def multiply(rows):
         return jnp.dot(ld[rows, :], ud[...], preferred_element_type=f32)
 
+    def multiply_part(rows, xi):
+        depth = pl.ds(pl.multiple_of(xi * 4 * B, 4 * B), 4 * B)
+        return jnp.dot(ld[rows, depth], ud[depth, :], preferred_element_type=f32)
+
     gz = {}
+    cs = {}
 
     def contribute(block, at):
         @pl.loop(0, NX)
@@ -258,67 +260,105 @@
         part_own[at] = multiply(mine)
         gz[at] = Copy(part_out.at[at], gz_in.at[at], "g", 1)
 
-    cs = {}
+    def begin(block, at):
+        @pl.loop(0, NX - 1)
+        def _(n):
+            spread_upper(ys[block], mod(x + n - 1, NX))
+
+        for rows, part in ((theirs, part_out), (mine, part_own)):
+            part[at] = (
+                multiply_part(rows, xs[-1]) + multiply_part(rows, x) + multiply_part(rows, xs[1])
+            )
 
     def settle(block, at):
         gz[at].arrived()
         c_out[at] = (part_own[at] + gz_in[at]).astype(bf16)
-        if block == 2:
-            for d in both:
-                for n in range(2):
-                    rows = pl.ds((2 * half_of[d] + n) * B, B)
-                    cs[d, n] = Copy(c_out.at[at, rows], c_relay.at[rows], "y", d)
-        else:
-            cs[block] = Copy(c_out.at[at], c_in.at[at], "y", block)
-
+        cs[block] = Copy(c_out.at[at], c_in.at[at], "y", block)
+
+    lz[1, 3, 0].arrived()
+    lz[-1, 3, 1].arrived()
+    spread_lower(zs[4])
+    for d in both:
+        xo[d, d, 1 - half_of[d]].arrived()
+        xo[d, -d, 1 - half_of[d]].arrived()
+    for d in both:
+        xf[d, 1].arrived()
+    contribute(1, 1)
     for d in both:
         xf[d, -1].arrived()
     contribute(-1, 0)
     for d in both:
-        for h in range(2):
-            xo[d, 2, h].arrived()
-    onward_x(2)
-    onward_x(0)
-    for d in both:
-        xf[d, 1].arrived()
+        onward_x(d, 2)
+    for d in both:
+        h = 1 - half_of[d]
+        own_late[d] = Copy(up.at[h, y, CL:], ubuf.at[y, x, h, CL:], "x", d)
+    for d in both:
+        onward_x(d, 0)
+    settle(1, 1)
     settle(-1, 0)
-    contribute(1, 1)
-    settle(1, 1)
+    for d in both:
+        xo[d, 2, 1 - half_of[d]].arrived()
+    begin(2, 2)
+
+    def chunk(d, p, m):
+        return p * 2 * B + half_of[d] * B + m * (B // 2)
 
     for d in both:
         xf[d, 2].arrived()
-    contribute(2, 2)
-    settle(2, 2)
+    spread_upper(ys[2], xs[2])
+    pieces = [pl.ds(p * 2 * B, 2 * B) for p in range(2)]
+
+    def piece_of(side, p):
+        return pl.ds(pl.multiple_of(side * HALF + p * 2 * B, 2 * B), 2 * B)
+
+    for p in range(2):
+        part_out[2, pieces[p]] += multiply_part(piece_of(1 - g, p), xs[2])
+    for p in range(2):
+        gz[2, p] = Copy(part_out.at[2, pieces[p]], gz_in.at[2, pieces[p]], "g", 1)
+    for p in range(2):
+        part_own[2, pieces[p]] += multiply_part(piece_of(g, p), xs[2])
+    for p in range(2):
+        gz[2, p].arrived()
+        c_out[2, pieces[p]] = (part_own[2, pieces[p]] + gz_in[2, pieces[p]]).astype(bf16)
+        for m in range(2):
+            for d in both:
+                rows = pl.ds(chunk(d, p, m), B // 2)
+                cs[d, p, m] = Copy(c_out.at[2, rows], c_relay.at[rows], "y", d)
+    for d in both:
+        xo[d, 0, 1 - half_of[d]].arrived()
+        own_late[d].arrived()
+    begin(0, 3)
     for d in both:
         xf[d, 0].arrived()
-    contribute(0, 3)
+    spread_upper(y, xs[2])
+    part_out[3] += multiply_part(theirs, xs[2])
+    part_own[3] += multiply_part(mine, xs[2])
+    gz[3] = Copy(part_out.at[3], gz_in.at[3], "g", 1)
 
     cf = {}
-    for n in range(2):
-        for d in both:
-            rows = pl.ds((2 * half_of[d] + n) * B, B)
-            cs[d, n].arrived()
-            cf[d, n] = Copy(c_relay.at[rows], c_in.at[2, rows], "y", d)
-    gz[3].arrived()
+    for p in range(2):
+        for m in range(2):
+            for d in both:
+                rows = pl.ds(chunk(d, p, m), B // 2)
+                cs[d, p, m].arrived()
+                cf[d, p, m] = Copy(c_relay.at[rows], c_in.at[2, rows], "y", d)
     cs[-1].arrived()
     cs[1].arrived()
+    gz[3].arrived()
     get_anc.wait()
     fin[...] = ancv[...] - (part_own[3] + gz_in[3] + c_in[0].astype(f32) + c_in[1].astype(f32))
     last = []
-    stores = []
-    for n in range(2):
-        for d in both:
-            begin = (2 * half_of[d] + n) * B
-            rows = pl.ds(begin, B)
-            there = pl.ds(pl.multiple_of(g * HALF + begin, B), B)
-            cf[d, n].arrived()
-            fin[rows] = fin[rows] - c_in[2, rows].astype(f32)
-            stores.append(local(fin.at[rows], out.at[there]))
-            last.append(Copy(fin.at[rows], out.at[there], "g", 1))
+    for p in range(2):
+        for m in range(2):
+            for d in both:
+                begins = chunk(d, p, m)
+                rows = pl.ds(begins, B // 2)
+                there = pl.ds(pl.multiple_of(g * HALF + begins, B // 2), B // 2)
+                cf[d, p, m].arrived()
+                out[there] = fin[rows] - c_in[2, rows].astype(f32)
+                last.append(Copy(out.at[there], out.at[there], "g", 1))
     for copy in last:
         copy.arrived()
-    for store in stores:
-        store.wait()
     for copy in started:
         copy.wait_send()
 
@@ -327,14 +367,14 @@
     ancestor, lower_panel, row_ids, row_counts, diag_inverse, upper_panel, col_ids, col_counts
 ):
     bf16, f32, i32 = jnp.bfloat16, jnp.float32, jnp.int32
-    anywhere = pl.BlockSpec(memory_space=pl.ANY)
+    anywhere = pl.BlockSpec(memory_space=pltpu.HBM)
     scalars = pl.BlockSpec(memory_space=pltpu.SMEM)
     vmem = pltpu.VMEM
     return pl.pallas_call(
         kernel,
-        out_shape=jax.ShapeDtypeStruct(ancestor.shape, f32),
+        out_shape=pltpu.VMEM(ancestor.shape, f32),
         in_specs=[scalars] * 4 + [anywhere] * 4,
-        out_specs=anywhere,
+        out_specs=pl.BlockSpec(memory_space=pltpu.VMEM),
         scratch_shapes=[
             vmem((2, RL, B, B), bf16),
             vmem((2, B, B), bf16),
@@ -362,11 +402,11 @@
             pltpu.SemaphoreType.DMA((N_LOCAL,)),
         ],
         compiler_params=pltpu.CompilerParams(
-            collective_id=0, has_side_effects=True, vmem_limit_bytes=60 * 1024 * 1024
+            collective_id=0, has_side_effects=True, vmem_limit_bytes=64_800_000
         ),
         name="schur_update",
     )(
-        row_ids[0], row_counts[0], col_ids[0], col_counts[0],
+        row_ids[0], row_counts.reshape(1, -1), col_ids.transpose(2, 0, 1), col_counts.reshape(1, -1),
         ancestor, lower_panel[0], diag_inverse[0],
         upper_panel[0].reshape(2, NY, 2 * CL, B, B),
     )

time: 100 us -> 80.6 us (0.81)
  Pallas kernels: 93.1 us -> 79.1 us
  local copies, waits for them, and re-layouts: 7.07 us -> 1.32 us
    pallas_call x1, Pallas kernels: 93.1 us -> 79.1 us  [on_device(): pl.pallas_call(kernel, out_shape=pltpu.VMEM(ancestor.shape, f32), in_spec...]
    squeeze x3 -> x0, local copies, waits for them, and re-layouts: 3.99 us -> none  [the longest x1 1.35 us: on_device(): col_ids[0]]
    unnamed x1, local copies, waits for them, and re-layouts: 3.08 us -> 1.32 us
where the time goes in v2:
time: 80.6 us; the launch traced here: 80.5 us
  Pallas kernels  79.1 us (98%)
  local copies, waits for them, and re-layouts  1.32 us (2%)
    pallas_call x1, Pallas kernels, on_device(): pl.pallas_call(kernel, out_shape=pltpu.VMEM(ancestor.shape, f32), in_spec...  79.1 us

profile of v2, /device:TPU:1, one launch (start us, length us, event | category | flops | bytes accessed | tf_op | source)
XLA Modules:
  0.0 80.5 jit_solution(3994408324197263965)
XLA Ops:
  0.0 79.1 %schur_update.1 = f32[1024,512]{1,0:T(8,128)S(1)} custom-call(s32[2,6]{1,0:T(2,128)} %bitcast.11, s32[1,2]{1,0:T(1,128)} %bitcast.12, s32[3,1,16]{2,1,0:T(1,128)} %bitcast.10, s32[1,16]{1,0:T(1,128)} %bitcast.13, f32[1024,512]{1,0:T(8,128)} %anc.1, bf16[2,6,128,128]{3,2,1,0:T(8,128)(2,1)} %bitcast.8, bf16[2,128,128]{2,1,0:T(8,128)(2,1)} %bitcast.9, ...), custom_call_target="tpu_custom_call" | custom-call | tf_op jit(solution)/shard_map/schur_update/pallas_call | solution.py:373
  79.1 1.3 %copy.10 = f32[1024,512]{1,0:T(8,128)} copy(f32[1024,512]{1,0:T(8,128)S(1)} %schur_update.1) | data formatting | bytes 4194304
